TPU v7x, 32 devices: a whole 2x2x4 slice. The times are simulated.
32 devices in a mesh: grp: 16 (over z, y, x), row: 2 (over core).
Axes of the slice: x: 2, y: 2, z: 4, core: 2. Of those that a mesh axis runs over, the one named last changes fastest.
Arguments:
- image_rows: bfloat16 [64, 16, 16, 512], P('grp', 'row'), may hold values from -6 to 6
- grad_out: bfloat16 [64, 16, 16, 512], P(('grp', 'row')), may hold values from -6 to 6
- code_ids: int32 [16384], P(('grp', 'row')), may hold values from 0 to 1023
- dead_flags: int32 [1024], replicated, may hold values from 0 to 1, as said below
- replace_ids: int32 [1024], replicated, may hold values from 0 to 16383
- latents: bfloat16 [16384, 256], P(('grp', 'row')), may hold values from -6 to 6
- codebook: float32 [1024, 256], P(('grp', 'row')), may hold values from -6 to 6
- norm1_gain: bfloat16 [512], replicated, may hold values from 0.5 to 1.5
- norm1_bias: bfloat16 [512], replicated, may hold values from -3 to 3
- conv1_kernel: bfloat16 [3, 3, 512, 512], replicated, may hold values from -0.09375 to 0.09375
- conv1_bias: bfloat16 [512], replicated, may hold values from -3 to 3
- norm2_gain: bfloat16 [512], replicated, may hold values from 0.5 to 1.5
- norm2_bias: bfloat16 [512], replicated, may hold values from -3 to 3
- conv2_kernel: bfloat16 [3, 3, 512, 512], replicated, may hold values from -0.09375 to 0.09375
- conv2_bias: bfloat16 [512], replicated, may hold values from -3 to 3
- norm3_gain: bfloat16 [512], replicated, may hold values from 0.5 to 1.5
- norm3_bias: bfloat16 [512], replicated, may hold values from -3 to 3
- query_weight: bfloat16 [512, 512], replicated, may hold values from -0.25 to 0.25
- query_bias: bfloat16 [512], replicated, may hold values from -3 to 3
- key_weight: bfloat16 [512, 512], replicated, may hold values from -0.25 to 0.25
- value_weight: bfloat16 [512, 512], replicated, may hold values from -0.25 to 0.25
- value_bias: bfloat16 [512], replicated, may hold values from -3 to 3
- out_weight: bfloat16 [512, 512], replicated, may hold values from -2 to 2
- out_bias: bfloat16 [512], replicated, may hold values from -3 to 3
Outputs:
- block_out: bfloat16 [64, 16, 16, 512], P(('grp', 'row'))
- input_grad: bfloat16 [64, 16, 16, 512], P('grp', 'row')
- norm1_gain_grad: float32 [512], replicated
- norm1_bias_grad: float32 [512], replicated
- conv1_kernel_grad: float32 [3, 3, 512, 512], replicated
- conv1_bias_grad: float32 [512], replicated
- norm2_gain_grad: float32 [512], replicated
- norm2_bias_grad: float32 [512], replicated
- conv2_kernel_grad: float32 [3, 3, 512, 512], replicated
- conv2_bias_grad: float32 [512], replicated
- norm3_gain_grad: float32 [512], replicated
- norm3_bias_grad: float32 [512], replicated
- query_weight_grad: float32 [512, 512], replicated
- query_bias_grad: float32 [512], replicated
- key_weight_grad: float32 [512, 512], replicated
- value_weight_grad: float32 [512, 512], replicated
- value_bias_grad: float32 [512], replicated
- out_weight_grad: float32 [512, 512], replicated
- out_bias_grad: float32 [512], replicated
- new_codebook: float32 [1024, 256], P(('grp', 'row'))
- usage: int32 [1024], replicated
- perplexity: float32 [], replicated
Inputs may be any that keep to these rules, and one draw needn't show every extreme that they name: `code_ids`: a code index. `dead_flags`: exactly 256 entries are 1, the others 0. `replace_ids`: a row of latents.
All inputs are finite; a program needn't handle non-finite values.
Results may differ from a plain program's by a relative error of at most 0.014.
The roundings to bfloat16 on the way count: a program that leaves them out, or rounds other values in their place, can miss the bound.
Values may be sent and summed in bfloat16 or wider, within the bound.
No kernel may reach another device: no remote copies, remote signals or barrier semaphores. Data moves between devices by JAX's collectives and lax.ppermute only.
A program may use at most 128 MiB of HBM per device.

v0:
```python
import jax
import jax.numpy as jnp
from jax import lax
from jax.sharding import PartitionSpec as P

G = 32
epsilon = 1e-06


def group_norm(source, scaling, offsets):
    images, height, across, channels = source.shape
    grouped = source.reshape(images, height * across, G, channels // G)
    middle = jnp.mean(grouped, axis=(1, 3), keepdims=True)
    centered = grouped - middle
    spread = jnp.mean(centered * centered, axis=(1, 3), keepdims=True)
    normed = (centered * lax.rsqrt(spread + epsilon)).reshape(images, height, across, channels)
    return normed * scaling + offsets


def norm_swish(source, scaling, offsets):
    return jax.nn.silu(group_norm(source, scaling, offsets))


def padded(source):
    return jnp.pad(source, ((0, 0), (1, 1), (1, 1), (0, 0)))


def conv_taps(source, kernel):
    images, height, across, channels = source.shape
    border = padded(source)
    summed = jnp.zeros((images, height, across, kernel.shape[3]), jnp.float32)
    for tap_row in range(3):
        for tap_col in range(3):
            window = border[:, tap_row : tap_row + height, tap_col : tap_col + across, :]
            summed = summed + lax.dot_general(
                window,
                kernel[tap_row, tap_col],
                (((3,), (0,)), ((), ())),
                preferred_element_type=jnp.float32,
            )
    return summed


def kernel_grad(source, upstream):
    images, height, across, channels = source.shape
    border = padded(source)
    pieces = []
    for tap_row in range(3):
        for tap_col in range(3):
            window = border[:, tap_row : tap_row + height, tap_col : tap_col + across, :]
            pieces.append(
                lax.dot_general(
                    window,
                    upstream,
                    (((0, 1, 2), (0, 1, 2)), ((), ())),
                    preferred_element_type=jnp.float32,
                )
            )
    return jnp.stack(pieces).reshape(3, 3, channels, upstream.shape[3])


def flip_kernel(kernel):
    return jnp.transpose(kernel[::-1, ::-1], (0, 1, 3, 2))


def local(
    image_rows,
    grad_out,
    code_ids,
    dead_flags,
    replace_ids,
    latents,
    codebook,
    norm1_gain,
    norm1_bias,
    conv1_kernel,
    conv1_bias,
    norm2_gain,
    norm2_bias,
    conv2_kernel,
    conv2_bias,
    norm3_gain,
    norm3_bias,
    query_weight,
    query_bias,
    key_weight,
    value_weight,
    value_bias,
    out_weight,
    out_bias,
):
    (
        first_gain,
        first_offset,
        first_bias,
        second_gain,
        second_offset,
        second_bias,
        third_gain,
        third_offset,
        query_offset,
        value_offset,
        out_offset,
    ) = [
        vector.astype(jnp.float32)
        for vector in (
            norm1_gain,
            norm1_bias,
            conv1_bias,
            norm2_gain,
            norm2_bias,
            conv2_bias,
            norm3_gain,
            norm3_bias,
            query_bias,
            value_bias,
            out_bias,
        )
    ]
    regrouped = lax.all_to_all(image_rows, "row", split_axis=0, concat_axis=1, tiled=True)
    images, height, across, channels = regrouped.shape
    positions = height * across
    pixels = images * positions
    key_scale = channels ** (-0.5)
    contract_rows = (((0,), (0,)), ((), ()))
    contract_cols = (((1,), (1,)), ((), ()))
    source = regrouped.astype(jnp.float32)
    first_active = norm_swish(source, first_gain, first_offset).astype(jnp.bfloat16)
    first_filtered = conv_taps(first_active, conv1_kernel) + first_bias
    second_active = norm_swish(first_filtered, second_gain, second_offset).astype(jnp.bfloat16)
    residual = source + (conv_taps(second_active, conv2_kernel) + second_bias)
    normed = (
        group_norm(residual, third_gain, third_offset)
        .astype(jnp.bfloat16)
        .reshape(pixels, channels)
    )
    queries = (
        (jnp.dot(normed, query_weight, preferred_element_type=jnp.float32) + query_offset)
        .astype(jnp.bfloat16)
        .reshape(images, positions, channels)
    )
    key_rows = (
        jnp.dot(normed, key_weight, preferred_element_type=jnp.float32)
        .astype(jnp.bfloat16)
        .reshape(images, positions, channels)
    )
    values = (
        (jnp.dot(normed, value_weight, preferred_element_type=jnp.float32) + value_offset)
        .astype(jnp.bfloat16)
        .reshape(images, positions, channels)
    )
    scores = (
        jnp.einsum("bnd,bmd->bnm", queries, key_rows, preferred_element_type=jnp.float32)
        * key_scale
    )
    peak_score = jnp.max(scores, axis=2, keepdims=True)
    lifted = jnp.exp(scores - peak_score)
    summed = jnp.sum(lifted, axis=2, keepdims=True)
    log_total = peak_score + jnp.log(summed)
    attention_low = (lifted / summed).astype(jnp.bfloat16)
    blended = (
        jnp.einsum("bnm,bmd->bnd", attention_low, values, preferred_element_type=jnp.float32)
        .astype(jnp.bfloat16)
        .reshape(pixels, channels)
    )
    projected = jnp.dot(blended, out_weight, preferred_element_type=jnp.float32) + out_offset
    block_out = (residual + projected.reshape(images, height, across, channels)).astype(
        jnp.bfloat16
    )
    upstream = grad_out.reshape(pixels, channels)
    out_bias_grad = jnp.sum(upstream.astype(jnp.float32), axis=0)
    out_weight_grad = lax.dot_general(
        blended, upstream, contract_rows, preferred_element_type=jnp.float32
    )
    grad_blended = (
        lax.dot_general(upstream, out_weight, contract_cols, preferred_element_type=jnp.float32)
        .astype(jnp.bfloat16)
        .reshape(images, positions, channels)
    )
    rescored = (
        jnp.einsum("bnd,bmd->bnm", queries, key_rows, preferred_element_type=jnp.float32)
        * key_scale
    )
    attention = jnp.exp(rescored - log_total)
    grad_values = (
        jnp.einsum(
            "bnm,bnd->bmd",
            attention.astype(jnp.bfloat16),
            grad_blended,
            preferred_element_type=jnp.float32,
        )
        .astype(jnp.bfloat16)
        .reshape(pixels, channels)
    )
    grad_attention = jnp.einsum(
        "bnd,bmd->bnm", grad_blended, values, preferred_element_type=jnp.float32
    )
    grad_scores = (
        attention * (grad_attention - jnp.sum(attention * grad_attention, axis=2, keepdims=True))
    ).astype(jnp.bfloat16)
    grad_queries = (
        (
            jnp.einsum("bnm,bmd->bnd", grad_scores, key_rows, preferred_element_type=jnp.float32)
            * key_scale
        )
        .astype(jnp.bfloat16)
        .reshape(pixels, channels)
    )
    grad_keys = (
        (
            jnp.einsum("bnm,bnd->bmd", grad_scores, queries, preferred_element_type=jnp.float32)
            * key_scale
        )
        .astype(jnp.bfloat16)
        .reshape(pixels, channels)
    )
    query_bias_grad = jnp.sum(grad_queries.astype(jnp.float32), axis=0)
    value_bias_grad = jnp.sum(grad_values.astype(jnp.float32), axis=0)
    query_weight_grad = lax.dot_general(
        normed, grad_queries, contract_rows, preferred_element_type=jnp.float32
    )
    key_weight_grad = lax.dot_general(
        normed, grad_keys, contract_rows, preferred_element_type=jnp.float32
    )
    value_weight_grad = lax.dot_general(
        normed, grad_values, contract_rows, preferred_element_type=jnp.float32
    )
    grad_normed = lax.dot_general(
        grad_queries, query_weight, contract_cols, preferred_element_type=jnp.float32
    )
    grad_normed = grad_normed + lax.dot_general(
        grad_keys, key_weight, contract_cols, preferred_element_type=jnp.float32
    )
    grad_normed = grad_normed + lax.dot_general(
        grad_values, value_weight, contract_cols, preferred_element_type=jnp.float32
    )
    skipped, third_pull = jax.vjp(group_norm, residual, third_gain, third_offset)
    grad_residual, third_gain_grad, third_offset_grad = third_pull(
        grad_normed.reshape(images, height, across, channels)
    )
    grad_residual = grad_residual + grad_out.astype(jnp.float32)
    grad_second_out = grad_residual.astype(jnp.bfloat16)
    second_bias_grad = jnp.sum(grad_second_out.astype(jnp.float32), axis=(0, 1, 2))
    conv2_kernel_grad = kernel_grad(second_active, grad_second_out)
    grad_second = conv_taps(grad_second_out, flip_kernel(conv2_kernel))
    skipped, second_pull = jax.vjp(norm_swish, first_filtered, second_gain, second_offset)
    grad_first_filtered, second_gain_grad, second_offset_grad = second_pull(grad_second)
    grad_first_out = grad_first_filtered.astype(jnp.bfloat16)
    first_bias_grad = jnp.sum(grad_first_out.astype(jnp.float32), axis=(0, 1, 2))
    conv1_kernel_grad = kernel_grad(first_active, grad_first_out)
    grad_first = conv_taps(grad_first_out, flip_kernel(conv1_kernel))
    skipped, first_pull = jax.vjp(norm_swish, source, first_gain, first_offset)
    grad_source, first_gain_grad, first_offset_grad = first_pull(grad_first)
    input_local = (grad_residual + grad_source).astype(jnp.bfloat16)
    input_grad = lax.all_to_all(input_local, "row", split_axis=1, concat_axis=0, tiled=True)
    code_range = jnp.arange(dead_flags.shape[0], dtype=jnp.int32)
    counts = jnp.sum((code_ids[:, None] == code_range[None, :]).astype(jnp.float32), axis=0)
    (
        first_gain_grad,
        first_offset_grad,
        conv1_kernel_grad,
        first_bias_grad,
        second_gain_grad,
        second_offset_grad,
        conv2_kernel_grad,
        second_bias_grad,
        counts,
        third_gain_grad,
        third_offset_grad,
        query_weight_grad,
        query_bias_grad,
        key_weight_grad,
        value_weight_grad,
        value_bias_grad,
        out_weight_grad,
        out_bias_grad,
    ) = lax.psum(
        (
            first_gain_grad,
            first_offset_grad,
            conv1_kernel_grad,
            first_bias_grad,
            second_gain_grad,
            second_offset_grad,
            conv2_kernel_grad,
            second_bias_grad,
            counts,
            third_gain_grad,
            third_offset_grad,
            query_weight_grad,
            query_bias_grad,
            key_weight_grad,
            value_weight_grad,
            value_bias_grad,
            out_weight_grad,
            out_bias_grad,
        ),
        ("grp", "row"),
    )
    shares = counts / jnp.sum(counts)
    perplexity = jnp.exp(-jnp.sum(shares * jnp.log(shares + 1e-10)))
    usage = counts.astype(jnp.int32)
    local_pixels = latents.shape[0]
    book_rows = codebook.shape[0]
    device_index = lax.axis_index(("grp", "row"))
    pixel_offset = device_index * local_pixels
    pixel_range = jnp.arange(local_pixels, dtype=jnp.int32)
    own_flags = lax.dynamic_slice_in_dim(dead_flags, device_index * book_rows, book_rows)
    wanted = replace_ids - pixel_offset
    chosen = (wanted[:, None] == pixel_range[None, :]).astype(jnp.bfloat16)
    fetched = lax.psum_scatter(
        jnp.dot(chosen, latents, preferred_element_type=jnp.float32),
        ("grp", "row"),
        scatter_dimension=0,
        tiled=True,
    )
    new_codebook = jnp.where(own_flags[:, None] == 1, fetched, codebook)
    return (
        block_out,
        input_grad,
        first_gain_grad,
        first_offset_grad,
        conv1_kernel_grad,
        first_bias_grad,
        second_gain_grad,
        second_offset_grad,
        conv2_kernel_grad,
        second_bias_grad,
        third_gain_grad,
        third_offset_grad,
        query_weight_grad,
        query_bias_grad,
        key_weight_grad,
        value_weight_grad,
        value_bias_grad,
        out_weight_grad,
        out_bias_grad,
        new_codebook,
        usage,
        perplexity,
    )


def solution(mesh):
    in_specs = (
        P("grp", "row", None, None),
        P(("grp", "row"), None, None, None),
        P(("grp", "row")),
        P(),
        P(),
        P(("grp", "row"), None),
        P(("grp", "row"), None),
        P(),
        P(),
        P(),
        P(),
        P(),
        P(),
        P(),
        P(),
        P(),
        P(),
        P(),
        P(),
        P(),
        P(),
        P(),
        P(),
        P(),
    )
    out_specs = (
        P(("grp", "row"), None, None, None),
        P("grp", "row", None, None),
        P(),
        P(),
        P(),
        P(),
        P(),
        P(),
        P(),
        P(),
        P(),
        P(),
        P(),
        P(),
        P(),
        P(),
        P(),
        P(),
        P(),
        P(("grp", "row"), None),
        P(),
        P(),
    )
    return jax.shard_map(local, mesh=mesh, in_specs=in_specs, out_specs=out_specs, check_vma=False)
```

profile of v0, /device:TPU:0, one launch (start us, length us, event | category | flops | bytes accessed | tf_op | source)
XLA Modules:
  0.0 556.4 jit_solution(8809578873958543179)
XLA Ops:
  7.2 3.6 all-to-all-start
  11.6 2.4 fusion
  40.6 5.3 reshape.298
  55.7 6.6 %copy.106 = bf16[3,3,512,512]{2,3,1,0:T(8,128)(2,1)} copy(bf16[3,3,512,512]{3,2,1,0:T(8,128)(2,1)} %param.37) | data formatting | bytes 9437184 | tf_op args[13]
  62.3 2.3 convolution_convert_fusion.2
  64.6 2.6 fusion.139
  68.8 6.1 %copy.103 = f32[2,256,32,16]{1,0,3,2:T(2,128)} copy(f32[2,256,32,16]{3,2,1,0:T(8,128)} %reshape.298) | data formatting | bytes 2097152 | tf_op jit(solution)/shard_map/reshape | solution.py:12
  74.9 2.6 fusion.141
  77.5 2.0 convolution_add_fusion.17
  82.6 2.5 copy.100
  85.1 2.9 reshape.297
  88.2 2.9 fusion.27
  91.6 2.8 reverse_bitcast_fusion.1
  102.1 1.9 multiply_reduce_fusion.1
  113.9 3.3 copy-done.13
  122.7 3.7 copy-done.12
  126.4 6.9 %copy.107 = bf16[3,3,512,512]{2,3,1,0:T(8,128)(2,1)} copy(bf16[3,3,512,512]{3,2,1,0:T(8,128)(2,1)} %param.33) | data formatting | bytes 9437184 | tf_op args[9]
  133.3 2.7 reverse_bitcast_fusion
  145.5 3.1 add_convert_fusion
  149.5 3.5 all-to-all-start.1
  155.8 44.5 %all-reduce.4 = (f32[512]{0:T(512)}, f32[512]{0:T(512)}, f32[512]{0:T(512)}, f32[512]{0:T(512)}, f32[512]{0:T(512)}, /*index=5*/f32[512]{0:T(512)}, f32[512]{0:T...) all-reduce(f32[512]{0:T(512)S(1)} %get-tuple-element.24, ...), channel_id=1, replica_groups=mesh['grp'=16,'row'=2] {'grp','row'}, use_global_device_ids=true, to_apply=%region_27.28 | all-reduce | flops 6656 | bytes 53248 | tf_op jit(solution)/shard_map/psum | solution.py:277
  205.7 325.8 %all-reduce.8.cloned.1.call-done = (f32[3,3,512,512]{3,2,1,0:T(8,128)}, f32[3,3,512,512]{3,2,1,0:T(8,128)}, f32[512,512]{1,0:T(8,128)}, f32[512,512]{1,0:T(8,128...) async-done(((f32[3,3,512,512]{3,2,1,0:T(8,128)}, f32[3,3,512,512]{3,2,1,0:T(8,128)}, f32[512,512]{1,0:T(8,128)}, f32[512,512]{1,0:T(8,128)}, f32[512,512]{1,0:T(8,128)}, ...) | async-done | bytes 23068688 | tf_op jit(solution)/shard_map/psum | solution.py:277
  531.5 8.8 %copy.191 = f32[3,3,512,512]{3,2,1,0:T(8,128)} copy(f32[3,3,512,512]{3,2,1,0:T(8,128)} %get-tuple-element.78) | data formatting | bytes 18874368
  540.3 4.1 copy.192
  (268 shorter events, 86.4 us)
Async XLA Ops:
  7.2 44.0 %copy-start = (bf16[512,512]{1,0:T(8,128)(2,1)S(1)}, bf16[512,512]{1,0:T(8,128)(2,1)}, u32[]{:S(2)}) copy-start(bf16[512,512]{1,0:T(8,128)(2,1)} %param.44) | copy-start | bytes 1572868
  7.2 8.3 %copy-start.31 = (bf16[512]{0:T(512)(128)(2,1)S(1)}, bf16[512]{0:T(512)(128)(2,1)}, u32[]{:S(2)}) copy-start(bf16[512]{0:T(512)(128)(2,1)} %param.32) | copy-start | bytes 3076
  7.2 9.3 %copy-start.32 = (bf16[512]{0:T(512)(128)(2,1)S(1)}, bf16[512]{0:T(512)(128)(2,1)}, u32[]{:S(2)}) copy-start(bf16[512]{0:T(512)(128)(2,1)} %param.35) | copy-start | bytes 3076
  7.2 9.3 %copy-start.33 = (bf16[512]{0:T(512)(128)(2,1)S(1)}, bf16[512]{0:T(512)(128)(2,1)}, u32[]{:S(2)}) copy-start(bf16[512]{0:T(512)(128)(2,1)} %param.34) | copy-start | bytes 3076
  7.2 7.6 %all-to-all-start = ((bf16[4,8,16,512]{3,2,1,0:T(8,128)(2,1)}), bf16[4,8,16,512]{3,2,1,0:T(8,128)(2,1)S(1)}, u32[]{:S(2)}, u32[]{:S(2)}) async-start(bf16[4,8,16,512]{3,2,1,0:T(8,128)(2,1)} %param.24), calls=%async_computation | async-start | bytes 1048576 | tf_op jit(solution)/shard_map/all_to_all | solution.py:120
  10.9 193.4 %reduce-scatter.2.cloned.1.call-start = ((), (), s32[]{:S(2)}) async-start(), calls=%async_computation.3 | async-start | bytes 1081344 | tf_op jit(solution)/shard_map/reduce_scatter | solution.py:311
  14.1 517.4 %all-reduce.8.cloned.1.call-start = ((), (), s32[]{:S(2)}) async-start(), calls=%async_computation.4 | async-start | bytes 46137344 | tf_op jit(solution)/shard_map/psum | solution.py:277
  26.3 5.4 copy-start.35
  30.8 6.0 %copy-start.5 = (f32[2,16,16,512]{3,2,1,0:T(8,128)}, f32[2,16,16,512]{3,2,1,0:T(8,128)S(1)}, u32[]{:S(2)}) copy-start(f32[2,16,16,512]{3,2,1,0:T(8,128)S(1)} %get-tuple-element.60) | copy-start | bytes 3145732
  31.7 6.6 %slice-start = ((s8[4718592]{0:T(1024)(128)(4,1)}), s8[4194304]{0:T(1024)(128)(4,1)S(1)}, s32[]{:S(2)}) async-start(s8[4718592]{0:T(1024)(128)(4,1)} %bitcast.513), calls=%async_computation.5 | async-start | bytes 8388608
  40.6 6.2 %copy-start.29 = (bf16[512]{0:T(512)(128)(2,1)S(1)}, bf16[512]{0:T(512)(128)(2,1)}, u32[]{:S(2)}) copy-start(bf16[512]{0:T(512)(128)(2,1)} %param.39) | copy-start | bytes 3076
  40.6 6.2 %copy-start.36 = (bf16[512]{0:T(512)(128)(2,1)S(1)}, bf16[512]{0:T(512)(128)(2,1)}, u32[]{:S(2)}) copy-start(bf16[512]{0:T(512)(128)(2,1)} %param.40) | copy-start | bytes 3076
  40.6 6.2 %copy-start.37 = (bf16[512]{0:T(512)(128)(2,1)S(1)}, bf16[512]{0:T(512)(128)(2,1)}, u32[]{:S(2)}) copy-start(bf16[512]{0:T(512)(128)(2,1)} %param.42) | copy-start | bytes 3076
  40.6 6.4 %copy-start.19 = (bf16[512,512]{1,0:T(8,128)(2,1)S(1)}, bf16[512,512]{1,0:T(8,128)(2,1)}, u32[]{:S(2)}) copy-start(bf16[512,512]{1,0:T(8,128)(2,1)} %param.43) | copy-start | bytes 1572868
  62.3 5.0 copy-start.9
  62.3 5.0 copy-start.17
  68.8 6.1 %copy-start.10 = (bf16[2,16,16,512]{3,2,1,0:T(8,128)(2,1)S(1)}, bf16[2,16,16,512]{3,2,1,0:T(8,128)(2,1)}, u32[]{:S(2)}) copy-start(bf16[2,16,16,512]{3,2,1,0:T(8,128)(2,1)} %copy-done.8) | copy-start | bytes 1572868
  139.6 5.9 %copy-start.16 = (bf16[2,16,16,512]{3,2,1,0:T(8,128)(2,1)S(1)}, bf16[2,16,16,512]{3,2,1,0:T(8,128)(2,1)}, u32[]{:S(2)}) copy-start(bf16[2,16,16,512]{3,2,1,0:T(8,128)(2,1)} %param.25) | copy-start | bytes 1572868
  145.5 10.0 %copy-start.30 = (s32[512]{0:T(512)S(1)}, s32[512]{0:T(512)}, u32[]{:S(2)}) copy-start(s32[512]{0:T(512)} %param.26) | copy-start | bytes 6148
  145.5 58.7 %copy-start.26 = (f32[32,256]{1,0:T(8,128)S(1)}, f32[32,256]{1,0:T(8,128)}, u32[]{:S(2)}) copy-start(f32[32,256]{1,0:T(8,128)} %param.30) | copy-start | bytes 98308
  149.5 5.2 all-to-all-start.1
  531.5 8.8 %copy-start.11 = (f32[3,3,512,512]{3,2,1,0:T(8,128)S(1)}, f32[3,3,512,512]{3,2,1,0:T(8,128)}, u32[]{:S(2)}) copy-start(f32[3,3,512,512]{3,2,1,0:T(8,128)} %get-tuple-element.82) | copy-start | bytes 28311556
  540.3 5.0 copy-start.23
  540.3 8.0 %copy-start.1 = (bf16[512,512]{1,0:T(8,128)(2,1)S(1)}, bf16[512,512]{1,0:T(8,128)(2,1)}, u32[]{:S(2)}) copy-start(bf16[512,512]{1,0:T(8,128)(2,1)} %param.44) | copy-start | bytes 1572868
  (25 other events, 74.5 us)
Sparse Core Ops, SparseCore 0:
  14.2 137.6 reduce-scatter.1
  160.6 370.8 all-reduce.7
where the time goes:
time: 564 us; the launch traced here: 556 us
  waiting for transfers between devices  326 us (58%)
  matrix products  69.9 us (12%)
  local copies, waits for them, and re-layouts  68.8 us (12%)
  blocking collectives  44.5 us (8%)
  other arithmetic  22.6 us (4%)
  between operations  17.2 us (3%)
  starting transfers between devices  7.2 us (1%)
    psum x1, waiting for transfers between devices, local(): lax.psum((first_gain_grad, first_offset_grad, conv1_kernel_grad, first_bi...  326 us
    psum x1, blocking collectives, local(): lax.psum((first_gain_grad, first_offset_grad, conv1_kernel_grad, first_bi...  44.5 us
    unnamed x98, local copies, waits for them, and re-layouts  41.5 us
    dot_general x36, matrix products, conv_taps(): lax.dot_general(window, kernel[tap_row, tap_col], (((3,), (0,)), ((), ())...  32.7 us
    reshape x2, local copies, waits for them, and re-layouts, group_norm(): grouped = source.reshape(images, height * across, G, channels // G)  11.4 us
  transfers between devices with their start and end apart: 4, of which 2 were waited for; matrix products, arithmetic and copies ran while one was open for 24% of the time, Pallas kernels for 0%

commit v1 on v0

--- a/solution.py
+++ b/solution.py
@@ -5,6 +5,12 @@
 
 G = 32
 epsilon = 1e-06
+
+
+def define_scenes(inputs):
+    f_now = lax.psum(inputs, "row")
+    n_now = lax.psum(f_now, "grp")
+    return n_now
 
 
 def group_norm(source, scaling, offsets):
@@ -274,7 +280,7 @@
         value_bias_grad,
         out_weight_grad,
         out_bias_grad,
-    ) = lax.psum(
+    ) = define_scenes(
         (
             first_gain_grad,
             first_offset_grad,
@@ -294,8 +300,7 @@
             value_bias_grad,
             out_weight_grad,
             out_bias_grad,
-        ),
-        ("grp", "row"),
+        )
     )
     shares = counts / jnp.sum(counts)
     perplexity = jnp.exp(-jnp.sum(shares * jnp.log(shares + 1e-10)))

time: 564 us -> 860 us (1.52)
  waiting for transfers between devices: 326 us -> 590 us
  blocking collectives: 44.5 us -> 84.3 us
    psum x1 -> x2, waiting for transfers between devices: 326 us -> 544 us  [the longest x1 469 us: define_scenes(): n_now = lax.psum(f_now, 'grp')]
    reduce_scatter x1, waiting for transfers between devices: 0.01 us -> 44 us  [local(): lax.psum_scatter(jnp.dot(chosen, latents, preferred_element_type=jnp.floa...]
    psum x1 -> x2, blocking collectives: 44.5 us -> 84.3 us  [the longest x1 80.9 us: define_scenes(): n_now = lax.psum(f_now, 'grp')]
    unnamed x98 -> x120, local copies, waits for them, and re-layouts: 41.5 us -> 41.7 us
  transfers between devices with their start and end apart: 4 -> 5, of which waited for: 2 -> 5; matrix products, arithmetic and copies ran while one was open for 24% -> 4% of each run, Pallas kernels for 0% -> 0%
where the time goes in v1:
time: 860 us; the launch traced here: 853 us
  waiting for transfers between devices  590 us (69%)
  blocking collectives  84.3 us (10%)
  local copies, waits for them, and re-layouts  69 us (8%)
  matrix products  61.6 us (7%)
  other arithmetic  21.9 us (3%)
  between operations  18.8 us (2%)
    psum x1, waiting for transfers between devices, define_scenes(): n_now = lax.psum(f_now, 'grp')  469 us
    psum x1, blocking collectives, define_scenes(): n_now = lax.psum(f_now, 'grp')  80.9 us
    psum x1, waiting for transfers between devices, define_scenes(): f_now = lax.psum(inputs, 'row')  75.5 us
    reduce_scatter x1, waiting for transfers between devices, local(): lax.psum_scatter(jnp.dot(chosen, latents, preferred_element_type=jnp.floa...  44 us
    unnamed x120, local copies, waits for them, and re-layouts  41.7 us
    dot_general x36, matrix products, conv_taps(): lax.dot_general(window, kernel[tap_row, tap_col], (((3,), (0,)), ((), ())...  25.6 us
  transfers between devices with their start and end apart: 5, of which 5 were waited for; matrix products, arithmetic and copies ran while one was open for 4% of the time, Pallas kernels for 0%

profile of v1, /device:TPU:0, one launch (start us, length us, event | category | flops | bytes accessed | tf_op | source)
XLA Modules:
  0.0 852.6 jit_solution(7964240179336301901)
XLA Ops:
  8.1 3.6 all-to-all-start
  32.3 5.3 reshape.298
  47.4 6.6 copy.106
  54.0 2.3 convolution_convert_fusion.2
  56.3 2.6 fusion.139
  60.4 6.1 copy.103
  66.4 2.5 fusion.141
  74.0 2.5 copy.100
  76.6 2.9 reshape.297
  79.7 2.9 fusion.27
  83.0 2.8 reverse_bitcast_fusion.1
  105.3 3.3 copy-done.14
  111.9 3.7 copy-done.13
  119.6 75.5 %all-reduce.13.cloned.1.call-done = (f32[3,3,512,512]{3,2,1,0:T(8,128)}, f32[3,3,512,512]{3,2,1,0:T(8,128)}, f32[512,512]{1,0:T(8,128)}, f32[512,512]{1,0:T(8,12...) async-done(((f32[3,3,512,512]{3,2,1,0:T(8,128)}, f32[3,3,512,512]{3,2,1,0:T(8,128)}, f32[512,512]{1,0:T(8,128)}, f32[512,512]{1,0:T(8,128)}, f32[512,512]{1,0:T(8,128)}, ...) | async-done | bytes 23068688 | tf_op jit(solution)/shard_map/psum | solution.py:11
  195.1 6.8 copy.107
  201.9 2.7 reverse_bitcast_fusion
  214.3 3.1 add_convert_fusion
  218.2 3.5 all-to-all-start.1
  224.5 3.4 all-reduce.6
  227.9 80.9 %all-reduce.4 = (f32[512]{0:T(512)}, f32[512]{0:T(512)}, f32[512]{0:T(512)}, f32[512]{0:T(512)}, f32[512]{0:T(512)}, /*index=5*/f32[512]{0:T(512)}, f32[512]{0:T...) all-reduce(f32[512]{0:T(512)S(1)} %get-tuple-element.50, ...), channel_id=1, replica_groups=mesh['grp'=16,'row'=2] {'grp'}, use_global_device_ids=true, to_apply=%region_28.29 | all-reduce | flops 6656 | bytes 53248 | tf_op jit(solution)/shard_map/psum | solution.py:12
  312.7 44.0 %reduce-scatter.2.cloned.1.call-done = f32[32,256]{1,0:T(8,128)} async-done(((f32[1024,256]{1,0:T(8,128)}), f32[32,256]{1,0:T(8,128)}) %reduce-scatter.2.cloned.1.call-update) | async-done | bytes 32784 | tf_op jit(solution)/shard_map/reduce_scatter | solution.py:316
  358.2 468.9 %all-reduce.11.cloned.1.call-done = (f32[3,3,512,512]{3,2,1,0:T(8,128)}, f32[3,3,512,512]{3,2,1,0:T(8,128)}, f32[512,512]{1,0:T(8,128)}, f32[512,512]{1,0:T(8,12...) async-done(((f32[3,3,512,512]{3,2,1,0:T(8,128)}, f32[3,3,512,512]{3,2,1,0:T(8,128)}, f32[512,512]{1,0:T(8,128)}, f32[512,512]{1,0:T(8,128)}, f32[512,512]{1,0:T(8,128)}, ...) | async-done | bytes 23068688 | tf_op jit(solution)/shard_map/psum | solution.py:12
  827.1 8.8 %copy.197 = f32[3,3,512,512]{3,2,1,0:T(8,128)} copy(f32[3,3,512,512]{3,2,1,0:T(8,128)} %get-tuple-element.96) | data formatting | bytes 18874368
  835.9 4.1 copy.198
  (294 shorter events, 85.2 us)
Async XLA Ops:
  8.0 34.8 %copy-start = (bf16[512,512]{1,0:T(8,128)(2,1)S(1)}, bf16[512,512]{1,0:T(8,128)(2,1)}, u32[]{:S(2)}) copy-start(bf16[512,512]{1,0:T(8,128)(2,1)} %param.44) | copy-start | bytes 1572868
  8.0 6.1 copy-start.41
  8.1 7.2 copy-start.42
  8.1 7.2 copy-start.43
  8.1 5.4 all-to-all-start
  11.7 183.4 %all-reduce.13.cloned.1.call-start = ((), (), s32[]{:S(2)}) async-start(), calls=%async_computation.5 | async-start | bytes 46137344 | tf_op jit(solution)/shard_map/psum | solution.py:11
  12.4 7.3 copy-start.31
  14.2 5.6 copy-start.27
  14.2 5.6 copy-start.34
  22.5 6.0 copy-start.5
  23.4 6.6 slice-start
  32.3 6.2 copy-start.38
  32.3 6.2 copy-start.46
  32.3 6.2 copy-start.47
  32.3 6.4 copy-start.20
  60.4 6.1 copy-start.11
  117.1 239.6 %reduce-scatter.2.cloned.1.call-start = ((), (), s32[]{:S(2)}) async-start(), calls=%async_computation.3 | async-start | bytes 1081344 | tf_op jit(solution)/shard_map/reduce_scatter | solution.py:316
  119.6 707.5 %all-reduce.11.cloned.1.call-start = ((), (), s32[]{:S(2)}) async-start(), calls=%async_computation.4 | async-start | bytes 46137344 | tf_op jit(solution)/shard_map/psum | solution.py:12
  208.3 5.9 copy-start.17
  214.2 10.0 %copy-start.40 = (s32[512]{0:T(512)S(1)}, s32[512]{0:T(512)}, u32[]{:S(2)}) copy-start(s32[512]{0:T(512)} %param.26) | copy-start | bytes 6148
  214.3 142.5 %copy-start.33 = (f32[32,256]{1,0:T(8,128)S(1)}, f32[32,256]{1,0:T(8,128)}, u32[]{:S(2)}) copy-start(f32[32,256]{1,0:T(8,128)} %param.30) | copy-start | bytes 98308
  218.2 5.2 all-to-all-start.1
  827.1 8.8 %copy-start.12 = (f32[3,3,512,512]{3,2,1,0:T(8,128)S(1)}, f32[3,3,512,512]{3,2,1,0:T(8,128)}, u32[]{:S(2)}) copy-start(f32[3,3,512,512]{3,2,1,0:T(8,128)} %get-tuple-element.100) | copy-start | bytes 28311556
  835.9 8.0 copy-start.1
  (37 other events, 110.4 us)
Sparse Core Ops, SparseCore 0:
  117.2 77.7 all-reduce.12
  201.5 625.5 all-reduce.10
Sparse Core Ops, SparseCore 1:
  120.5 236.1 reduce-scatter.1
